TPU v7x, 32 devices: a whole 2x2x4 slice. The times are simulated.
32 devices in a mesh: rep: 2 (over y), pair: 8 (over z, x), samp: 2 (over core).
Axes of the slice: x: 2, y: 2, z: 4, core: 2. Of those that a mesh axis runs over, the one named last changes fastest.
Arguments:
- dosage: bfloat16 [128, 4096], P(('rep', 'pair', 'samp')), parts along dimension 0, may hold values from 0 to 2
- phenotype: bfloat16 [2, 128], P(None, ('rep', 'pair', 'samp')), parts along dimension 1, may hold values from -6 to 6
- perms: int32 [2, 64], replicated, may hold values from 0 to 63, each once within a row
- pairs: int32 [8, 2], replicated, may hold values from 0 to 7
Outputs:
- stat: bfloat16 [16, 4, 512, 512], P(('rep', 'pair'), None, None, 'samp'), parts along dimension 0
There are 2 independent parts, one for each index of `rep`. A program takes and returns all parts, laid end to end along the dimension named above; an argument that names none is the same for every part. Nothing has to cross between parts.
Inputs may be any that keep to these rules, and one draw needn't show every extreme that they name: `perms`: each row is a permutation of the samples. `pairs`: panel ids; a panel may appear in many blocks.
All inputs are finite; a program needn't handle non-finite values.
Results may differ from a plain program's by a relative error of at most 0.02.
Values may be sent and summed in bfloat16 or wider, within the bound.
A program may use at most 64 MiB of HBM per device.

v0:
```python
import jax
import jax.numpy as jnp
from jax import lax
from jax.sharding import PartitionSpec as P

PANEL = 512


def finish(prod, ya, yb_half, marg_a, marg_b_half, ysum, count):
    value = prod - ya[:, :, None] * marg_b_half[None, None, :] / count
    value = value - marg_a[None, :, None] * yb_half[:, None, :] / count
    value = value + marg_a[None, :, None] * marg_b_half[None, None, :] * ysum[:, None, None] / (
        count * count
    )
    return (value / jnp.sqrt(count)).astype(jnp.bfloat16)[None]


def permuted(whole_y, perms, sample_ids):
    picked = whole_y[:, perms[:, sample_ids]]
    return picked.reshape(-1, sample_ids.shape[0])


def on_device(dosage, phenotype, perms, pairs):
    s_dev = dosage.shape[0]
    pair_count = lax.axis_size("pair")
    samp_count = lax.axis_size("samp")
    grouped = dosage.reshape(s_dev, -1, PANEL)
    picked = jnp.take(grouped, pairs.reshape(-1), axis=1).reshape(s_dev, pairs.shape[0], 2 * PANEL)
    whole_y = lax.all_gather(phenotype, ("pair", "samp"), axis=1, tiled=True).astype(jnp.float32)
    count = jnp.float32(whole_y.shape[1])
    received = lax.all_to_all(picked, "pair", split_axis=1, concat_axis=0, tiled=True).reshape(
        pair_count * s_dev, 2 * PANEL
    )
    geno_a = received[:, :PANEL]
    geno_b = received[:, PANEL:]
    full_a = lax.all_gather(geno_a, "samp", axis=0, tiled=True)
    part_b = lax.all_to_all(geno_b, "samp", split_axis=1, concat_axis=0, tiled=True)
    rows = jnp.arange(full_a.shape[0], dtype=jnp.int32)
    group = rows // received.shape[0]
    inner = rows % received.shape[0]
    sample_ids = inner // s_dev * samp_count * s_dev + group * s_dev + inner % s_dev
    yperm = permuted(whole_y, perms, sample_ids)
    scaled = (yperm[:, :, None] * full_a[None].astype(jnp.float32)).astype(jnp.bfloat16)
    prod_half = jnp.einsum("ksi,sj->kij", scaled, part_b, preferred_element_type=jnp.float32)
    ya = jnp.sum(scaled, axis=1, dtype=jnp.float32)
    yb_half = jnp.einsum(
        "ks,sj->kj", yperm, part_b.astype(jnp.float32), precision=lax.Precision.HIGHEST
    )
    marg_a = jnp.sum(full_a, axis=0, dtype=jnp.float32)
    marg_b_half = jnp.sum(part_b, axis=0, dtype=jnp.float32)
    ysum = jnp.sum(yperm, axis=1)
    return finish(prod_half, ya, yb_half, marg_a, marg_b_half, ysum, count)


def solution(mesh):
    placed = (P(("rep", "pair", "samp"), None), P(None, ("rep", "pair", "samp")), P(), P())
    return jax.shard_map(
        on_device,
        mesh=mesh,
        in_specs=placed,
        out_specs=P(("rep", "pair"), None, None, "samp"),
        check_vma=False,
    )
```

profile of v0, /device:TPU:0, one launch (start us, length us, event | category | flops | bytes accessed | tf_op | source)
XLA Modules:
  0.0 43.8 jit_solution(8418153733974152815)
XLA Ops:
  0.0 0.0 copy-start
  0.0 0.7 %compare_and_fusion = pred[8,2]{0,1:T(4,128)(4,1)S(1)} fusion(s32[8,2]{0,1:T(2,128)} %param.7), kind=kLoop, calls=%fused_computation.23 | loop fusion | flops 96 | bytes 80 | tf_op jit(solution)/shard_map/jit(_take)/and | solution.py:28
  0.7 0.8 %copy.24 = s32[8,2]{1,0:T(8,128)S(1)} copy(s32[8,2]{0,1:T(2,128)} %param.7) | data formatting | bytes 128 | tf_op args[3]
  1.4 0.1 reshape.239
  1.5 0.0 copy-done
  1.6 0.6 %gather_fusion.2 = bf16[16,4,512]{2,1,0:T(4,128)(2,1)S(1)} fusion(bf16[4,8,512]{2,0,1:T(4,128)(2,1)S(1)} %bitcast.49, s32[1024]{0:T(1024)S(1)} %pad_clamp_fusion), kind=kCustom, calls=%fused_computation.2 | custom fusion | bytes 131136 | tf_op jit(solution)/shard_map/jit(_take)/gather | solution.py:28
  2.2 0.1 broadcast_in_dim.16
  2.2 0.7 %broadcast_select_fusion = bf16[4,8,1024]{2,0,1:T(4,128)(2,1)} fusion(bf16[4,8,1024]{2,0,1:T(4,128)(2,1)S(1)} %bitcast.53, pred[8,1024]{1,0:T(8,128)(4,1)S(1)} %bitcast.61), kind=kLoop, calls=%fused_computation.12 | loop fusion | flops 32768 | bytes 139264 | tf_op jit(solution)/shard_map/jit(_take)/select_n | solution.py:28
  2.9 7.3 %all-to-all-start = ((bf16[4,8,1024]{2,0,1:T(4,128)(2,1)}), bf16[4,8,1024]{2,0,1:T(4,128)(2,1)S(1)}, u32[]{:S(2)}, u32[]{:S(2)}) async-start(bf16[4,8,1024]{2,0,1:T(4,128)(2,1)} %broadcast_select_fusion), calls=%async_computation | async-start | bytes 131072 | tf_op jit(solution)/shard_map/all_to_all | solution.py:31
  10.2 0.8 %copy.21 = s32[2,64]{0,1:T(8,128)S(1)} copy(s32[2,64]{1,0:T(2,128)} %param.6) | data formatting | bytes 1024 | tf_op args[2]
  11.0 0.6 %gather_fusion = s32[64,2]{1,0:T(8,128)S(1)} fusion(s32[2,64]{0,1:T(8,128)S(1)} %copy.21, s32[1024]{0:T(1024)S(1)} %pad_clamp_fusion.2), kind=kCustom, calls=%fused_computation | custom fusion | bytes 1280 | tf_op jit(solution)/shard_map/gather | solution.py:19
  11.6 0.1 copy.22
  11.7 0.1 reshape.252
  11.8 22.0 %all-gather = bf16[16,4,2]{1,2,0:T(2,128)(2,1)S(1)} all-gather(bf16[1,4,2]{1,2,0:T(2,128)(2,1)} %bitcast.65), channel_id=1, replica_groups=mesh['rep'=2,'pair'=8,'samp'=2] {'pair','samp'}, dimensions={0}, use_global_device_ids=true | all-gather | bytes 272 | tf_op jit(solution)/shard_map/all_gather | solution.py:29
  33.8 0.2 copy.27
  34.0 0.7 %gather_fusion.3 = bf16[128,2]{1,0:T(8,128)(2,1)S(1)} fusion(bf16[2,64]{0,1:T(8,128)(2,1)S(1)} %bitcast.57, s32[1024]{0:T(1024)S(1)} %pad_clamp_fusion.1), kind=kCustom, calls=%fused_computation.3 | custom fusion | bytes 1536 | tf_op jit(solution)/shard_map/gather | solution.py:19
  34.7 0.1 copy.26
  34.8 0.7 %gather_fusion.1 = f32[128,2]{1,0:T(8,128)S(1)} fusion(f32[2,64]{0,1:T(8,128)S(1)} %convert_element_type.22, s32[1024]{0:T(1024)S(1)} %pad_clamp_fusion.1), kind=kCustom, calls=%fused_computation.1 | custom fusion | bytes 2560 | tf_op jit(solution)/shard_map/gather | solution.py:19
  35.4 0.1 copy.23
  35.5 0.1 bitcast_reduce_fusion
  35.6 0.1 mul.115
  35.7 0.0 all-to-all-done
  35.7 1.9 %all_gather.7 = bf16[64,512]{1,0:T(8,128)(2,1)S(1)} all-gather(bf16[32,512]{1,0:T(8,128)(2,1)S(1)} %get-tuple-element.5), channel_id=1, replica_groups=mesh['rep'=2,'pair'=8,'samp'=2] {'samp'}, dimensions={0}, use_global_device_ids=true | all-gather | bytes 98304 | tf_op jit(solution)/shard_map/all_gather | solution.py:36
  37.7 3.7 %all_to_all.34 = bf16[32,2,256]{2,0,1:T(8,128)(2,1)S(1)} all-to-all(bf16[32,2,256]{2,0,1:T(8,128)(2,1)S(1)} %bitcast.54), channel_id=1, replica_groups=mesh['rep'=2,'pair'=8,'samp'=2] {'samp'}, dimensions={1} | all-to-all | bytes 65536 | tf_op jit(solution)/shard_map/all_to_all | solution.py:37
  41.4 0.1 fusion.9
  41.5 0.1 convert_reduce_fusion
  41.7 0.1 broadcast_multiply_fusion
  41.8 2.0 %fusion = bf16[1,4,512,256]{3,2,1,0:T(8,128)(2,1)} fusion(bf16[64,256,1]{1,0,2:T(8,128)(2,1)S(1)} %bitcast.51, f32[4]{0:T(128)S(1)} %mul.115, f32[512,256]{1,0:T(8,128)S(1)} %broadcast_multiply_fusion, f32[4,256]{1,0:T(4,128)S(1)} %fusion.9, f32[512]{0:T(512)S(1)} %convert_reduce_fusion.2, f32[256]{0:T(256)S(1)} %convert_reduce_fusion.1, ...), kind=kOutput, calls=%fused_computation.5 | convolution fusion | flops 73138176 | bytes 1753104 | tf_op jit(solution)/shard_map/ksi,sj->kij/dot_general | solution.py:44
  (13 shorter events, 0.2 us)
Async XLA Ops:
  0.0 1.5 %copy-start = (bf16[4,4096]{1,0:T(4,128)(2,1)S(1)}, bf16[4,4096]{1,0:T(4,128)(2,1)}, u32[]{:S(2)}) copy-start(bf16[4,4096]{1,0:T(4,128)(2,1)} %param.4) | copy-start | bytes 98308
  2.9 32.8 %all-to-all-start = ((bf16[4,8,1024]{2,0,1:T(4,128)(2,1)}), bf16[4,8,1024]{2,0,1:T(4,128)(2,1)S(1)}, u32[]{:S(2)}, u32[]{:S(2)}) async-start(bf16[4,8,1024]{2,0,1:T(4,128)(2,1)} %broadcast_select_fusion), calls=%async_computation | async-start | bytes 131072 | tf_op jit(solution)/shard_map/all_to_all | solution.py:31
where the time goes:
time: 44.2 us; the launch traced here: 43.8 us
  blocking collectives  27.6 us (62%)
  starting transfers between devices  7.28 us (16%)
  local copies, waits for them, and re-layouts  4.91 us (11%)
  matrix products  2.11 us (5%)
  other arithmetic  1.85 us (4%)
    all_gather x1, blocking collectives, on_device(): lax.all_gather(phenotype, ('pair', 'samp'), axis=1, tiled=True)  22 us
    all_to_all x1, starting transfers between devices, on_device(): lax.all_to_all(picked, 'pair', split_axis=1, concat_axis=0, tiled=True)  7.28 us
    all_to_all x1, blocking collectives, on_device(): lax.all_to_all(geno_b, 'samp', split_axis=1, concat_axis=0, tiled=True)  3.75 us
    gather x6, local copies, waits for them, and re-layouts, permuted(): picked = whole_y[:, perms[:, sample_ids]]  2.21 us
    dot_general x1, matrix products, on_device(): jnp.einsum('ksi,sj->kij', scaled, part_b, preferred_element_type=jnp.floa...  1.99 us
    all_gather x1, blocking collectives, on_device(): full_a = lax.all_gather(geno_a, 'samp', axis=0, tiled=True)  1.85 us
    unnamed x5, local copies, waits for them, and re-layouts  1.73 us
  transfers between devices with their start and end apart: 1, of which 0 were waited for; matrix products, arithmetic and copies ran while one was open for 8% of the time, Pallas kernels for 0%

commit v1 on v0

v1 whole, which is shorter than its diff:
```python
import functools

import jax
import jax.numpy as jnp
from jax import lax
from jax.experimental import pallas as pl
from jax.experimental.pallas import tpu as pltpu
from jax.sharding import PartitionSpec as P

PANEL = 512
LANES = 128


def exchange(n, samp, pairs_ref, dosage_ref, pheno_ref, out_ref, send_buf, send_sem, recv_sem):
    half = PANEL // samp
    me = lax.axis_index("pair") * samp + lax.axis_index("samp")
    s_dev = dosage_ref.shape[0]

    barrier = pltpu.get_barrier_semaphore()

    def greet(d, carry):
        dest = lax.rem(me + d, n)
        pl.semaphore_signal(
            barrier, inc=1, device_id={"pair": dest // samp, "samp": dest % samp},
            device_id_type=pl.DeviceIdType.MESH,
        )
        return carry

    lax.fori_loop(1, n, greet, 0)

    row = lax.broadcasted_iota(jnp.int32, (s_dev, s_dev), 0)
    col = lax.broadcasted_iota(jnp.int32, (s_dev, s_dev), 1)
    lane = lax.broadcasted_iota(jnp.int32, (s_dev, LANES), 1)
    tail = jnp.zeros((s_dev, LANES), jnp.float32)
    for g in range(pheno_ref.shape[0]):
        values = pheno_ref[...].astype(jnp.float32)[g : g + 1, :]
        column = jnp.sum(jnp.where(row == col, values, 0.0), axis=1, keepdims=True)
        tail = jnp.where(lane == g, column, tail)
    tail = tail.astype(jnp.bfloat16)

    panels = dosage_ref.shape[1] // PANEL

    def fill(b, carry):
        first = jnp.full((s_dev, PANEL), pairs_ref[0, b], jnp.int32)
        second = jnp.full((s_dev, PANEL), pairs_ref[1, b], jnp.int32)

        def pick(p, kept):
            at = p * PANEL if isinstance(p, int) else pl.multiple_of(p * PANEL, PANEL)
            panel = dosage_ref[:, pl.ds(at, PANEL)].astype(jnp.float32)
            return jnp.where(first == p, panel, kept[0]), jnp.where(second == p, panel, kept[1])

        kept = (jnp.zeros((s_dev, PANEL), jnp.float32),) * 2
        if panels <= 16:
            for p in range(panels):
                kept = pick(p, kept)
        else:
            kept = lax.fori_loop(0, panels, pick, kept)
        geno_a, geno_b = (x.astype(jnp.bfloat16) for x in kept)
        for c in range(samp):
            send_buf[b * samp + c, :, :PANEL] = geno_a
            send_buf[b * samp + c, :, PANEL : PANEL + half] = geno_b[:, c * half : (c + 1) * half]
            send_buf[b * samp + c, :, PANEL + half :] = tail
        return carry

    lax.fori_loop(0, n // samp, fill, 0)
    pl.semaphore_wait(barrier, n - 1)

    own = pltpu.make_async_copy(send_buf.at[me], out_ref.at[me], recv_sem)
    own.start()

    def send(d, carry):
        dest = lax.rem(me + d, n)
        pltpu.make_async_remote_copy(
            src_ref=send_buf.at[dest],
            dst_ref=out_ref.at[me],
            send_sem=send_sem,
            recv_sem=recv_sem,
            device_id={"pair": dest // samp, "samp": dest % samp},
            device_id_type=pl.DeviceIdType.MESH,
        ).start()
        return carry

    lax.fori_loop(1, n, send, 0)
    pltpu.make_async_copy(out_ref, out_ref, recv_sem).wait()
    rest = send_buf.at[pl.ds(0, n - 1)]
    pltpu.make_async_copy(rest, rest, send_sem).wait()


def statistics(half, perms_ref, recv_ref, out_ref, tiles, sems):
    n, s_dev, _ = recv_ref.shape
    count = n * s_dev
    genes = tiles.shape[0] // perms_ref.shape[0]
    perms_n = perms_ref.shape[0]
    rows = jnp.concatenate([recv_ref[i].astype(jnp.float32) for i in range(n)], axis=0)
    geno_a = rows[:, :PANEL]
    geno_b = rows[:, PANEL : PANEL + half]
    pheno = rows[:, PANEL + half :].T[:8].astype(jnp.bfloat16)

    a_twice = jnp.concatenate([geno_a, geno_a], axis=0).T
    a_low = a_twice.astype(jnp.bfloat16)

    marg_b = jnp.sum(geno_b, axis=0, keepdims=True)
    centred = (geno_b - marg_b * (1.0 / count)) * (1.0 / count**0.5)
    high = centred.astype(jnp.bfloat16)
    low = (centred - high.astype(jnp.float32)).astype(jnp.bfloat16)
    b_split = jnp.concatenate([high, low], axis=0)

    sample = lax.broadcasted_iota(jnp.int32, (count, 2 * count), 0)
    picked = []
    for r in range(perms_n):
        order = perms_ref[r : r + 1, :]
        order = jnp.concatenate([order, order], axis=1)
        hot = jnp.where(sample == order, 1.0, 0.0).astype(jnp.bfloat16)
        picked.append(jnp.dot(pheno, hot, preferred_element_type=jnp.float32))
    slopes = [
        jnp.dot(picked[r].astype(jnp.bfloat16), b_split, preferred_element_type=jnp.float32)
        * (-1.0 / count)
        for r in range(perms_n)
    ]
    copies = []
    for k in range(genes * perms_n):
        g, r = k // perms_n, k % perms_n
        y = picked[r][g : g + 1, :]
        scaled = (a_twice * y).astype(jnp.bfloat16)
        slope = slopes[r][g : g + 1, :]
        slope_high = slope.astype(jnp.bfloat16).astype(jnp.float32)
        slope_low = slope - slope_high
        slope_rows = jnp.concatenate(
            [
                jnp.broadcast_to(slope_high, (count, half)),
                jnp.broadcast_to(slope_low, (count, half)),
            ],
            axis=0,
        ).astype(jnp.bfloat16)
        left = jnp.concatenate([scaled, a_low], axis=1)
        right = jnp.concatenate([b_split, slope_rows], axis=0)
        tiles[k] = jnp.dot(left, right, preferred_element_type=jnp.float32).astype(jnp.bfloat16)
        copy = pltpu.make_async_copy(tiles.at[k], out_ref.at[0, k], sems.at[k])
        copy.start()
        copies.append(copy)
    for copy in copies:
        copy.wait()


def on_device(dosage, phenotype, perms, pairs):
    samp = lax.axis_size("samp")
    n = lax.axis_size("pair") * samp
    half = PANEL // samp
    s_dev = dosage.shape[0]
    width = PANEL + half + LANES
    kinds = phenotype.shape[0] * perms.shape[0]
    vmem = pl.BlockSpec(memory_space=pltpu.VMEM)
    smem = pl.BlockSpec(memory_space=pltpu.SMEM)
    received = pl.pallas_call(
        functools.partial(exchange, n, samp),
        out_shape=jax.ShapeDtypeStruct((n, s_dev, width), jnp.bfloat16),
        in_specs=[smem, vmem, vmem],
        out_specs=vmem,
        scratch_shapes=[
            pltpu.VMEM((n, s_dev, width), jnp.bfloat16),
            pltpu.SemaphoreType.DMA,
            pltpu.SemaphoreType.DMA,
        ],
        compiler_params=pltpu.CompilerParams(collective_id=0, has_side_effects=True),
        name="exchange",
    )(pairs.T, dosage, phenotype)
    return pl.pallas_call(
        functools.partial(statistics, half),
        out_shape=jax.ShapeDtypeStruct((1, kinds, PANEL, half), jnp.bfloat16),
        in_specs=[vmem, vmem],
        out_specs=pl.BlockSpec(memory_space=pl.ANY),
        scratch_shapes=[
            pltpu.VMEM((kinds, PANEL, half), jnp.bfloat16),
            pltpu.SemaphoreType.DMA((kinds,)),
        ],
        name="statistics",
    )(perms, received)


def solution(mesh):
    placed = (P(("rep", "pair", "samp"), None), P(None, ("rep", "pair", "samp")), P(), P())
    return jax.shard_map(
        on_device,
        mesh=mesh,
        in_specs=placed,
        out_specs=P(("rep", "pair"), None, None, "samp"),
        check_vma=False,
    )
```

time: 44.2 us -> 13.2 us (0.30)
  blocking collectives: 27.6 us -> 0 us
  Pallas kernels: 0 us -> 13 us
  starting transfers between devices: 7.28 us -> 0 us
  local copies, waits for them, and re-layouts: 4.91 us -> 0 us
  matrix products: 2.11 us -> 0 us
  other arithmetic: 1.85 us -> 0 us
    all_gather x2 -> x0, blocking collectives: 23.8 us -> none  [the longest x1 22 us: on_device(): lax.all_gather(phenotype, ('pair', 'samp'), axis=1, tiled=True)]
    pallas_call x0 -> x2, Pallas kernels: none -> 13 us  [the longest x1 10.5 us: on_device(): pl.pallas_call(functools.partial(exchange, n, samp), out_shape=jax.ShapeD...]
    all_to_all x1 -> x0, starting transfers between devices: 7.28 us -> none  [on_device(): lax.all_to_all(picked, 'pair', split_axis=1, concat_axis=0, tiled=True)]
    all_to_all x1 -> x0, blocking collectives: 3.75 us -> none  [on_device(): lax.all_to_all(geno_b, 'samp', split_axis=1, concat_axis=0, tiled=True)]
    gather x7 -> x0, local copies, waits for them, and re-layouts: 2.82 us -> none  [the longest x6 2.21 us: permuted(): picked = whole_y[:, perms[:, sample_ids]]]
    dot_general x2 -> x0, matrix products: 2.11 us -> none  [the longest x1 1.99 us: on_device(): jnp.einsum('ksi,sj->kij', scaled, part_b, preferred_element_type=jnp.floa...]
    unnamed x5 -> x0, local copies, waits for them, and re-layouts: 1.73 us -> none
    select_n x4 -> x0, other arithmetic: 0.72 us -> none  [the longest x2 0.7 us: on_device(): jnp.take(grouped, pairs.reshape(-1), axis=1)]
  transfers between devices with their start and end apart: 1 -> 0, of which waited for: 0 -> 0; matrix products, arithmetic and copies ran while one was open for 8% -> 0% of each run, Pallas kernels for 0% -> 0%
where the time goes in v1:
time: 13.2 us; the launch traced here: 13 us
  Pallas kernels  13 us (98%)
    pallas_call x1, Pallas kernels, on_device(): pl.pallas_call(functools.partial(exchange, n, samp), out_shape=jax.ShapeD...  10.5 us
    pallas_call x1, Pallas kernels, on_device(): pl.pallas_call(functools.partial(statistics, half), out_shape=jax.ShapeDt...  2.52 us

profile of v1, /device:TPU:0, one launch (start us, length us, event | category | flops | bytes accessed | tf_op | source)
XLA Modules:
  0.0 13.0 jit_solution(10267085517930546055)
XLA Ops:
  0.0 10.5 %exchange.1.recv_ref = bf16[16,4,896]{2,1,0:T(4,128)(2,1)} custom-call(s32[2,8]{1,0:T(2,128)} %bitcast.1, bf16[4,4096]{1,0:T(4,128)(2,1)} %dosage_ref.1, bf16[2,4]{1,0:T(2,128)(2,1)} %pheno_ref.1), custom_call_target="tpu_custom_call" | custom-call | tf_op jit(solution)/shard_map/exchange/pallas_call | solution.py:154
  10.5 2.5 %statistics.1 = bf16[1,4,512,256]{3,2,1,0:T(8,128)(2,1)} custom-call(s32[2,64]{1,0:T(2,128)} %perms_ref.1, bf16[16,4,896]{2,1,0:T(4,128)(2,1)} %exchange.1.recv_ref), custom_call_target="tpu_custom_call" | custom-call | tf_op jit(solution)/shard_map/statistics/pallas_call | solution.py:167

commit v2 on v1

--- a/solution.py
+++ b/solution.py
@@ -11,22 +11,44 @@
 LANES = 128
 
 
-def exchange(n, samp, pairs_ref, dosage_ref, pheno_ref, out_ref, send_buf, send_sem, recv_sem):
+def partner(me, m, n):
+    if n & (n - 1):
+        return lax.rem(me + m, n)
+    dest, weight = 0, 1
+    while weight < n:
+        dest = dest + (me // weight + m // weight) % 2 * weight
+        weight *= 2
+    return dest
+
+
+def exchange(
+    n, samp, pairs_hbm, dosage_hbm, pheno_hbm, out_ref,
+    pairs_ref, dosage_ref, pheno_ref, send_buf, in_sems, send_sem, recv_sem,
+):
     half = PANEL // samp
     me = lax.axis_index("pair") * samp + lax.axis_index("samp")
     s_dev = dosage_ref.shape[0]
 
+    inputs = [
+        pltpu.make_async_copy(dosage_hbm, dosage_ref, in_sems.at[0]),
+        pltpu.make_async_copy(pheno_hbm, pheno_ref, in_sems.at[1]),
+        pltpu.make_async_copy(pairs_hbm, pairs_ref, in_sems.at[2]),
+    ]
+    for copy in inputs:
+        copy.start()
     barrier = pltpu.get_barrier_semaphore()
 
-    def greet(d, carry):
-        dest = lax.rem(me + d, n)
+    def greet(i, carry):
+        dest = partner(me, n - 1 - i, n)
         pl.semaphore_signal(
             barrier, inc=1, device_id={"pair": dest // samp, "samp": dest % samp},
             device_id_type=pl.DeviceIdType.MESH,
         )
         return carry
 
-    lax.fori_loop(1, n, greet, 0)
+    lax.fori_loop(0, n - 1, greet, 0, unroll=n <= 16)
+    for copy in inputs:
+        copy.wait()
 
     row = lax.broadcasted_iota(jnp.int32, (s_dev, s_dev), 0)
     col = lax.broadcasted_iota(jnp.int32, (s_dev, s_dev), 1)
@@ -65,11 +87,8 @@
     lax.fori_loop(0, n // samp, fill, 0)
     pl.semaphore_wait(barrier, n - 1)
 
-    own = pltpu.make_async_copy(send_buf.at[me], out_ref.at[me], recv_sem)
-    own.start()
-
-    def send(d, carry):
-        dest = lax.rem(me + d, n)
+    def send(i, carry):
+        dest = partner(me, n - 1 - i, n)
         pltpu.make_async_remote_copy(
             src_ref=send_buf.at[dest],
             dst_ref=out_ref.at[me],
@@ -80,7 +99,8 @@
         ).start()
         return carry
 
-    lax.fori_loop(1, n, send, 0)
+    lax.fori_loop(0, n - 1, send, 0, unroll=n <= 16)
+    pltpu.make_async_copy(send_buf.at[me], out_ref.at[me], recv_sem).start()
     pltpu.make_async_copy(out_ref, out_ref, recv_sem).wait()
     rest = send_buf.at[pl.ds(0, n - 1)]
     pltpu.make_async_copy(rest, rest, send_sem).wait()
@@ -150,18 +170,26 @@
     width = PANEL + half + LANES
     kinds = phenotype.shape[0] * perms.shape[0]
     vmem = pl.BlockSpec(memory_space=pltpu.VMEM)
-    smem = pl.BlockSpec(memory_space=pltpu.SMEM)
+    hbm = pl.BlockSpec(memory_space=pltpu.HBM)
+    kept_bytes = 4 * n * s_dev * width + 2 * dosage.size + (2 << 20)
+    work_bytes = 64 * n * s_dev * PANEL + 4 * kinds * PANEL * half + (8 << 20)
     received = pl.pallas_call(
         functools.partial(exchange, n, samp),
         out_shape=jax.ShapeDtypeStruct((n, s_dev, width), jnp.bfloat16),
-        in_specs=[smem, vmem, vmem],
-        out_specs=vmem,
+        in_specs=[hbm, hbm, hbm],
+        out_specs=pl.BlockSpec(memory_space=pl.ANY),
         scratch_shapes=[
+            pltpu.SMEM((2, pairs.shape[0]), jnp.int32),
+            pltpu.VMEM(dosage.shape, dosage.dtype),
+            pltpu.VMEM(phenotype.shape, phenotype.dtype),
             pltpu.VMEM((n, s_dev, width), jnp.bfloat16),
+            pltpu.SemaphoreType.DMA((3,)),
             pltpu.SemaphoreType.DMA,
             pltpu.SemaphoreType.DMA,
         ],
-        compiler_params=pltpu.CompilerParams(collective_id=0, has_side_effects=True),
+        compiler_params=pltpu.CompilerParams(
+            collective_id=0, has_side_effects=True, vmem_limit_bytes=min(kept_bytes, 60 << 20)
+        ),
         name="exchange",
     )(pairs.T, dosage, phenotype)
     return pl.pallas_call(
@@ -173,6 +201,7 @@
             pltpu.VMEM((kinds, PANEL, half), jnp.bfloat16),
             pltpu.SemaphoreType.DMA((kinds,)),
         ],
+        compiler_params=pltpu.CompilerParams(vmem_limit_bytes=min(work_bytes, 60 << 20)),
         name="statistics",
     )(perms, received)
 

time: 13.2 us -> 13.5 us (1.023)
  local copies, waits for them, and re-layouts: 0 us -> 1.44 us
  Pallas kernels: 13 us -> 11.9 us
    unnamed x0 -> x8, local copies, waits for them, and re-layouts: none -> 1.44 us
    pallas_call x1, Pallas kernels: 2.52 us -> 1.6 us  [on_device(): pl.pallas_call(functools.partial(statistics, half), out_shape=jax.ShapeDt...]
    pallas_call x1, Pallas kernels: 10.5 us -> 10.3 us  [on_device(): pl.pallas_call(functools.partial(exchange, n, samp), out_shape=jax.ShapeD...]
where the time goes in v2:
time: 13.5 us; the launch traced here: 13.3 us
  Pallas kernels  11.9 us (88%)
  local copies, waits for them, and re-layouts  1.44 us (11%)
    pallas_call x1, Pallas kernels, on_device(): pl.pallas_call(functools.partial(exchange, n, samp), out_shape=jax.ShapeD...  10.3 us
    pallas_call x1, Pallas kernels, on_device(): pl.pallas_call(functools.partial(statistics, half), out_shape=jax.ShapeDt...  1.6 us
    unnamed x8, local copies, waits for them, and re-layouts  1.44 us

profile of v2, /device:TPU:0, one launch (start us, length us, event | category | flops | bytes accessed | tf_op | source)
XLA Modules:
  0.0 13.3 jit_solution(17054544314306863314)
XLA Ops:
  0.0 0.0 copy-start.1
  0.0 0.0 copy-start.3
  0.0 0.7 %copy-done.1 = s32[8,2]{0,1:T(2,128)S(1)} copy-done((s32[8,2]{0,1:T(2,128)S(1)}, s32[8,2]{0,1:T(2,128)}, u32[]{:S(2)}) %copy-start.1) | copy-done | bytes 88
  0.7 0.0 copy-done.3
  0.7 0.0 copy-start
  0.7 0.8 %copy-done = bf16[4,4096]{1,0:T(4,128)(2,1)S(1)} copy-done((bf16[4,4096]{1,0:T(4,128)(2,1)S(1)}, bf16[4,4096]{1,0:T(4,128)(2,1)}, u32[]{:S(2)}) %copy-start) | copy-done | bytes 32792
  1.4 0.0 copy-start.2
  1.4 10.3 %exchange.1.recv_ref = bf16[16,4,896]{2,1,0:T(4,128)(2,1)S(1)} custom-call(s32[2,8]{1,0:T(2,128)S(1)} %bitcast.1, bf16[4,4096]{1,0:T(4,128)(2,1)S(1)} %copy-done, bf16[2,4]{1,0:T(2,128)(2,1)S(1)} %copy-done.3), custom_call_target="tpu_custom_call" | custom-call | tf_op jit(solution)/shard_map/exchange/pallas_call | solution.py:176
  11.7 0.0 copy-done.2
  11.7 1.6 %statistics.1 = bf16[1,4,512,256]{3,2,1,0:T(8,128)(2,1)} custom-call(s32[2,64]{1,0:T(2,128)S(1)} %copy-done.2, bf16[16,4,896]{2,1,0:T(4,128)(2,1)S(1)} %exchange.1.recv_ref), custom_call_target="tpu_custom_call" | custom-call | tf_op jit(solution)/shard_map/statistics/pallas_call | solution.py:195
Async XLA Ops:
  0.0 0.7 %copy-start.1 = (s32[8,2]{0,1:T(2,128)S(1)}, s32[8,2]{0,1:T(2,128)}, u32[]{:S(2)}) copy-start(s32[8,2]{0,1:T(2,128)} %param.7) | copy-start | bytes 196
  0.0 0.7 %copy-start.3 = (bf16[2,4]{1,0:T(2,128)(2,1)S(1)}, bf16[2,4]{1,0:T(2,128)(2,1)}, u32[]{:S(2)}) copy-start(bf16[2,4]{1,0:T(2,128)(2,1)} %pheno_hbm.1) | copy-start | bytes 52
  0.7 0.8 %copy-start = (bf16[4,4096]{1,0:T(4,128)(2,1)S(1)}, bf16[4,4096]{1,0:T(4,128)(2,1)}, u32[]{:S(2)}) copy-start(bf16[4,4096]{1,0:T(4,128)(2,1)} %dosage_hbm.1) | copy-start | bytes 98308
  1.4 10.3 %copy-start.2 = (s32[2,64]{1,0:T(2,128)S(1)}, s32[2,64]{1,0:T(2,128)}, u32[]{:S(2)}) copy-start(s32[2,64]{1,0:T(2,128)} %perms_ref.1) | copy-start | bytes 1540

commit v3 on v2

--- a/solution.py
+++ b/solution.py
@@ -191,7 +191,7 @@
             collective_id=0, has_side_effects=True, vmem_limit_bytes=min(kept_bytes, 60 << 20)
         ),
         name="exchange",
-    )(pairs.T, dosage, phenotype)
+    )(*(pltpu.with_memory_space_constraint(x, pltpu.HBM) for x in (pairs.T, dosage, phenotype)))
     return pl.pallas_call(
         functools.partial(statistics, half),
         out_shape=jax.ShapeDtypeStruct((1, kinds, PANEL, half), jnp.bfloat16),

time: 13.5 us -> 12 us (0.89)
  local copies, waits for them, and re-layouts: 1.44 us -> 0.01 us
    unnamed x8 -> x2, local copies, waits for them, and re-layouts: 1.44 us -> 0.01 us
where the time goes in v3:
time: 12 us; the launch traced here: 11.8 us
  Pallas kernels  11.8 us (98%)
    pallas_call x1, Pallas kernels, on_device(): pl.pallas_call(functools.partial(exchange, n, samp), out_shape=jax.ShapeD...  10.2 us
    pallas_call x1, Pallas kernels, on_device(): pl.pallas_call(functools.partial(statistics, half), out_shape=jax.ShapeDt...  1.6 us

profile of v3, /device:TPU:0, one launch (start us, length us, event | category | flops | bytes accessed | tf_op | source)
XLA Modules:
  0.0 11.8 jit_solution(14269839427962338906)
XLA Ops:
  0.0 0.0 copy-start
  0.0 10.2 %exchange.1.recv_ref = bf16[16,4,896]{2,1,0:T(4,128)(2,1)S(1)} custom-call(s32[2,8]{1,0:T(2,128)} %bitcast.1, bf16[4,4096]{1,0:T(4,128)(2,1)} %dosage_hbm.1, bf16[2,4]{1,0:T(2,128)(2,1)} %pheno_hbm.1), custom_call_target="tpu_custom_call" | custom-call | tf_op jit(solution)/shard_map/exchange/pallas_call | solution.py:176
  10.2 0.0 copy-done
  10.2 1.6 %statistics.1 = bf16[1,4,512,256]{3,2,1,0:T(8,128)(2,1)} custom-call(s32[2,64]{1,0:T(2,128)S(1)} %copy-done, bf16[16,4,896]{2,1,0:T(4,128)(2,1)S(1)} %exchange.1.recv_ref), custom_call_target="tpu_custom_call" | custom-call | tf_op jit(solution)/shard_map/statistics/pallas_call | solution.py:195
Async XLA Ops:
  0.0 10.2 %copy-start = (s32[2,64]{1,0:T(2,128)S(1)}, s32[2,64]{1,0:T(2,128)}, u32[]{:S(2)}) copy-start(s32[2,64]{1,0:T(2,128)} %perms_ref.1) | copy-start | bytes 1540

commit v4 on v3

--- a/solution.py
+++ b/solution.py
@@ -61,45 +61,71 @@
     tail = tail.astype(jnp.bfloat16)
 
     panels = dosage_ref.shape[1] // PANEL
-
-    def fill(b, carry):
-        first = jnp.full((s_dev, PANEL), pairs_ref[0, b], jnp.int32)
-        second = jnp.full((s_dev, PANEL), pairs_ref[1, b], jnp.int32)
+    pair_me, samp_me = lax.axis_index("pair"), lax.axis_index("samp")
+    pair_n = n // samp
+    small = panels <= 16
+    if small:
+        whole = dosage_ref[...].astype(jnp.float32)
+
+    def fill(i):
+        b = partner(pair_me, pair_n - 1 - i, pair_n)
+        first = jnp.full((s_dev, LANES), pairs_ref[0, b], jnp.int32)
+        second = jnp.full((s_dev, LANES), pairs_ref[1, b], jnp.int32)
+        tiles = PANEL // LANES
 
         def pick(p, kept):
-            at = p * PANEL if isinstance(p, int) else pl.multiple_of(p * PANEL, PANEL)
-            panel = dosage_ref[:, pl.ds(at, PANEL)].astype(jnp.float32)
-            return jnp.where(first == p, panel, kept[0]), jnp.where(second == p, panel, kept[1])
-
-        kept = (jnp.zeros((s_dev, PANEL), jnp.float32),) * 2
-        if panels <= 16:
+            if small:
+                found = [whole[:, p * PANEL + t * LANES :][:, :LANES] for t in range(tiles)]
+            else:
+                panel = dosage_ref[:, pl.ds(pl.multiple_of(p * PANEL, PANEL), PANEL)]
+                found = [
+                    panel[:, t * LANES : (t + 1) * LANES].astype(jnp.float32) for t in range(tiles)
+                ]
+            in_a, in_b = first == p, second == p
+            return (
+                tuple(jnp.where(in_a, x, old) for x, old in zip(found, kept[0])),
+                tuple(jnp.where(in_b, x, old) for x, old in zip(found, kept[1])),
+            )
+
+        kept = ((jnp.zeros((s_dev, LANES), jnp.float32),) * tiles,) * 2
+        if small:
             for p in range(panels):
                 kept = pick(p, kept)
         else:
             kept = lax.fori_loop(0, panels, pick, kept)
-        geno_a, geno_b = (x.astype(jnp.bfloat16) for x in kept)
+        geno_a, geno_b = (jnp.concatenate(x, axis=1).astype(jnp.bfloat16) for x in kept)
         for c in range(samp):
             send_buf[b * samp + c, :, :PANEL] = geno_a
             send_buf[b * samp + c, :, PANEL : PANEL + half] = geno_b[:, c * half : (c + 1) * half]
             send_buf[b * samp + c, :, PANEL + half :] = tail
-        return carry
-
-    lax.fori_loop(0, n // samp, fill, 0)
-    pl.semaphore_wait(barrier, n - 1)
-
-    def send(i, carry):
-        dest = partner(me, n - 1 - i, n)
+
+    def send(b, c):
         pltpu.make_async_remote_copy(
-            src_ref=send_buf.at[dest],
+            src_ref=send_buf.at[b * samp + c],
             dst_ref=out_ref.at[me],
             send_sem=send_sem,
             recv_sem=recv_sem,
-            device_id={"pair": dest // samp, "samp": dest % samp},
+            device_id={"pair": b, "samp": c},
             device_id_type=pl.DeviceIdType.MESH,
         ).start()
+
+    fill(0)
+    pl.semaphore_wait(barrier, n - 1)
+
+    def step(i, carry):
+        fill(i + 1)
+        b = partner(pair_me, pair_n - 1 - i, pair_n)
+        for c in range(samp):
+            send(b, c)
         return carry
 
-    lax.fori_loop(0, n - 1, send, 0, unroll=n <= 16)
+    if small:
+        for i in range(pair_n - 1):
+            step(i, 0)
+    else:
+        lax.fori_loop(0, pair_n - 1, step, 0)
+    for c in range(1, samp):
+        send(pair_me, lax.rem(samp_me + c, samp))
     pltpu.make_async_copy(send_buf.at[me], out_ref.at[me], recv_sem).start()
     pltpu.make_async_copy(out_ref, out_ref, recv_sem).wait()
     rest = send_buf.at[pl.ds(0, n - 1)]

time: 12 us -> 11.9 us (level)
  no operation moved by 1% of the time
where the time goes in v4:
time: 11.9 us; the launch traced here: 11.7 us
  Pallas kernels  11.7 us (98%)
    pallas_call x1, Pallas kernels, on_device(): pl.pallas_call(functools.partial(exchange, n, samp), out_shape=jax.ShapeD...  10.1 us
    pallas_call x1, Pallas kernels, on_device(): pl.pallas_call(functools.partial(statistics, half), out_shape=jax.ShapeDt...  1.6 us

profile of v4, /device:TPU:0, one launch (start us, length us, event | category | flops | bytes accessed | tf_op | source)
XLA Modules:
  0.0 11.7 jit_solution(7299297746767123687)
XLA Ops:
  0.0 0.0 copy-start
  0.0 10.1 %exchange.1.recv_ref = bf16[16,4,896]{2,1,0:T(4,128)(2,1)S(1)} custom-call(s32[2,8]{1,0:T(2,128)} %bitcast.1, bf16[4,4096]{1,0:T(4,128)(2,1)} %dosage_hbm.1, bf16[2,4]{1,0:T(2,128)(2,1)} %pheno_hbm.1), custom_call_target="tpu_custom_call" | custom-call | tf_op jit(solution)/shard_map/exchange/pallas_call | solution.py:202
  10.1 0.0 copy-done
  10.1 1.6 %statistics.1 = bf16[1,4,512,256]{3,2,1,0:T(8,128)(2,1)} custom-call(s32[2,64]{1,0:T(2,128)S(1)} %copy-done, bf16[16,4,896]{2,1,0:T(4,128)(2,1)S(1)} %exchange.1.recv_ref), custom_call_target="tpu_custom_call" | custom-call | tf_op jit(solution)/shard_map/statistics/pallas_call | solution.py:221
Async XLA Ops:
  0.0 10.1 %copy-start = (s32[2,64]{1,0:T(2,128)S(1)}, s32[2,64]{1,0:T(2,128)}, u32[]{:S(2)}) copy-start(s32[2,64]{1,0:T(2,128)} %perms_ref.1) | copy-start | bytes 1540

commit v5 on v4

--- a/solution.py
+++ b/solution.py
@@ -9,6 +9,7 @@
 
 PANEL = 512
 LANES = 128
+CHUNKS = 2
 
 
 def partner(me, m, n):
@@ -22,8 +23,8 @@
 
 
 def exchange(
-    n, samp, pairs_hbm, dosage_hbm, pheno_hbm, out_ref,
-    pairs_ref, dosage_ref, pheno_ref, send_buf, in_sems, send_sem, recv_sem,
+    n, samp, pairs_hbm, dosage_hbm, pheno_hbm, perms_hbm, out_ref, y_ref, hot_ref,
+    pairs_ref, perms_ref, dosage_ref, pheno_ref, send_buf, own_y, in_sems, send_sem, recv_sem, y_send, y_recv,
 ):
     half = PANEL // samp
     me = lax.axis_index("pair") * samp + lax.axis_index("samp")
@@ -33,6 +34,7 @@
         pltpu.make_async_copy(dosage_hbm, dosage_ref, in_sems.at[0]),
         pltpu.make_async_copy(pheno_hbm, pheno_ref, in_sems.at[1]),
         pltpu.make_async_copy(pairs_hbm, pairs_ref, in_sems.at[2]),
+        pltpu.make_async_copy(perms_hbm, perms_ref, in_sems.at[3]),
     ]
     for copy in inputs:
         copy.start()
@@ -50,15 +52,12 @@
     for copy in inputs:
         copy.wait()
 
-    row = lax.broadcasted_iota(jnp.int32, (s_dev, s_dev), 0)
-    col = lax.broadcasted_iota(jnp.int32, (s_dev, s_dev), 1)
-    lane = lax.broadcasted_iota(jnp.int32, (s_dev, LANES), 1)
-    tail = jnp.zeros((s_dev, LANES), jnp.float32)
-    for g in range(pheno_ref.shape[0]):
-        values = pheno_ref[...].astype(jnp.float32)[g : g + 1, :]
-        column = jnp.sum(jnp.where(row == col, values, 0.0), axis=1, keepdims=True)
-        tail = jnp.where(lane == g, column, tail)
-    tail = tail.astype(jnp.bfloat16)
+    lane = lax.broadcasted_iota(jnp.int32, own_y.shape, 1)
+    values = pheno_ref[...].astype(jnp.float32)
+    placed = jnp.zeros(own_y.shape, jnp.float32)
+    for i in range(s_dev):
+        placed = jnp.where(lane == me * s_dev + i, values[:, i : i + 1], placed)
+    own_y[...] = placed.astype(jnp.bfloat16)
 
     panels = dosage_ref.shape[1] // PANEL
     pair_me, samp_me = lax.axis_index("pair"), lax.axis_index("samp")
@@ -97,7 +96,6 @@
         for c in range(samp):
             send_buf[b * samp + c, :, :PANEL] = geno_a
             send_buf[b * samp + c, :, PANEL : PANEL + half] = geno_b[:, c * half : (c + 1) * half]
-            send_buf[b * samp + c, :, PANEL + half :] = tail
 
     def send(b, c):
         pltpu.make_async_remote_copy(
@@ -108,6 +106,14 @@
             device_id={"pair": b, "samp": c},
             device_id_type=pl.DeviceIdType.MESH,
         ).start()
+        pltpu.make_async_remote_copy(
+            src_ref=own_y,
+            dst_ref=y_ref.at[me],
+            send_sem=y_send,
+            recv_sem=y_recv,
+            device_id={"pair": b, "samp": c},
+            device_id_type=pl.DeviceIdType.MESH,
+        ).start()
 
     fill(0)
     pl.semaphore_wait(barrier, n - 1)
@@ -127,20 +133,32 @@
     for c in range(1, samp):
         send(pair_me, lax.rem(samp_me + c, samp))
     pltpu.make_async_copy(send_buf.at[me], out_ref.at[me], recv_sem).start()
+    pltpu.make_async_copy(own_y, y_ref.at[me], y_recv).start()
+
+    count = hot_ref.shape[1]
+    sample = lax.broadcasted_iota(jnp.int32, (count, 2 * count), 0)
+    for r in range(perms_ref.shape[0]):
+        order = perms_ref[r : r + 1, :]
+        order = jnp.concatenate([order, order], axis=1)
+        hot_ref[r] = jnp.where(sample == order, 1.0, 0.0).astype(jnp.bfloat16)
+
     pltpu.make_async_copy(out_ref, out_ref, recv_sem).wait()
-    rest = send_buf.at[pl.ds(0, n - 1)]
-    pltpu.make_async_copy(rest, rest, send_sem).wait()
-
-
-def statistics(half, perms_ref, recv_ref, out_ref, tiles, sems):
+    pltpu.make_async_copy(y_ref, y_ref, y_recv).wait()
+    for buf, sem in ((send_buf, send_sem), (y_ref, y_send)):
+        rest = buf.at[pl.ds(0, n - 1)]
+        pltpu.make_async_copy(rest, rest, sem).wait()
+
+
+def statistics(half, recv_ref, y_ref, hot_ref, out_ref, tiles, sems):
     n, s_dev, _ = recv_ref.shape
     count = n * s_dev
-    genes = tiles.shape[0] // perms_ref.shape[0]
-    perms_n = perms_ref.shape[0]
+    perms_n = hot_ref.shape[0]
+    genes = tiles.shape[0] // perms_n
     rows = jnp.concatenate([recv_ref[i].astype(jnp.float32) for i in range(n)], axis=0)
     geno_a = rows[:, :PANEL]
     geno_b = rows[:, PANEL : PANEL + half]
-    pheno = rows[:, PANEL + half :].T[:8].astype(jnp.bfloat16)
+    pheno = jnp.sum(y_ref[...].astype(jnp.float32), axis=0)[:, :count]
+    pheno = jnp.concatenate([pheno] * (8 // genes), axis=0).astype(jnp.bfloat16)
 
     a_twice = jnp.concatenate([geno_a, geno_a], axis=0).T
     a_low = a_twice.astype(jnp.bfloat16)
@@ -151,13 +169,9 @@
     low = (centred - high.astype(jnp.float32)).astype(jnp.bfloat16)
     b_split = jnp.concatenate([high, low], axis=0)
 
-    sample = lax.broadcasted_iota(jnp.int32, (count, 2 * count), 0)
-    picked = []
-    for r in range(perms_n):
-        order = perms_ref[r : r + 1, :]
-        order = jnp.concatenate([order, order], axis=1)
-        hot = jnp.where(sample == order, 1.0, 0.0).astype(jnp.bfloat16)
-        picked.append(jnp.dot(pheno, hot, preferred_element_type=jnp.float32))
+    picked = [
+        jnp.dot(pheno, hot_ref[r], preferred_element_type=jnp.float32) for r in range(perms_n)
+    ]
     slopes = [
         jnp.dot(picked[r].astype(jnp.bfloat16), b_split, preferred_element_type=jnp.float32)
         * (-1.0 / count)
@@ -180,10 +194,16 @@
         ).astype(jnp.bfloat16)
         left = jnp.concatenate([scaled, a_low], axis=1)
         right = jnp.concatenate([b_split, slope_rows], axis=0)
-        tiles[k] = jnp.dot(left, right, preferred_element_type=jnp.float32).astype(jnp.bfloat16)
-        copy = pltpu.make_async_copy(tiles.at[k], out_ref.at[0, k], sems.at[k])
-        copy.start()
-        copies.append(copy)
+        for part in range(CHUNKS):
+            at = pl.ds(part * PANEL // CHUNKS, PANEL // CHUNKS)
+            block = left[part * PANEL // CHUNKS : (part + 1) * PANEL // CHUNKS]
+            value = jnp.dot(block, right, preferred_element_type=jnp.float32)
+            tiles[k, at] = value.astype(jnp.bfloat16)
+            copy = pltpu.make_async_copy(
+                tiles.at[k, at], out_ref.at[0, k, at], sems.at[k * CHUNKS + part]
+            )
+            copy.start()
+            copies.append(copy)
     for copy in copies:
         copy.wait()
 
@@ -193,23 +213,33 @@
     n = lax.axis_size("pair") * samp
     half = PANEL // samp
     s_dev = dosage.shape[0]
-    width = PANEL + half + LANES
+    count = n * s_dev
+    width = PANEL + half
+    y_shape = (phenotype.shape[0], pl.cdiv(n * s_dev, LANES) * LANES)
     kinds = phenotype.shape[0] * perms.shape[0]
     vmem = pl.BlockSpec(memory_space=pltpu.VMEM)
     hbm = pl.BlockSpec(memory_space=pltpu.HBM)
-    kept_bytes = 4 * n * s_dev * width + 2 * dosage.size + (2 << 20)
+    kept_bytes = 4 * n * s_dev * width + 2 * dosage.size + 16 * count * count + (2 << 20)
     work_bytes = 64 * n * s_dev * PANEL + 4 * kinds * PANEL * half + (8 << 20)
     received = pl.pallas_call(
         functools.partial(exchange, n, samp),
-        out_shape=jax.ShapeDtypeStruct((n, s_dev, width), jnp.bfloat16),
-        in_specs=[hbm, hbm, hbm],
-        out_specs=pl.BlockSpec(memory_space=pl.ANY),
+        out_shape=[
+            jax.ShapeDtypeStruct((n, s_dev, width), jnp.bfloat16),
+            jax.ShapeDtypeStruct((n, *y_shape), jnp.bfloat16),
+            jax.ShapeDtypeStruct((perms.shape[0], count, 2 * count), jnp.bfloat16),
+        ],
+        in_specs=[hbm] * 4,
+        out_specs=[pl.BlockSpec(memory_space=pl.ANY)] * 2 + [vmem],
         scratch_shapes=[
             pltpu.SMEM((2, pairs.shape[0]), jnp.int32),
+            pltpu.VMEM(perms.shape, jnp.int32),
             pltpu.VMEM(dosage.shape, dosage.dtype),
             pltpu.VMEM(phenotype.shape, phenotype.dtype),
             pltpu.VMEM((n, s_dev, width), jnp.bfloat16),
-            pltpu.SemaphoreType.DMA((3,)),
+            pltpu.VMEM(y_shape, jnp.bfloat16),
+            pltpu.SemaphoreType.DMA((4,)),
+            pltpu.SemaphoreType.DMA,
+            pltpu.SemaphoreType.DMA,
             pltpu.SemaphoreType.DMA,
             pltpu.SemaphoreType.DMA,
         ],
@@ -217,19 +247,19 @@
             collective_id=0, has_side_effects=True, vmem_limit_bytes=min(kept_bytes, 60 << 20)
         ),
         name="exchange",
-    )(*(pltpu.with_memory_space_constraint(x, pltpu.HBM) for x in (pairs.T, dosage, phenotype)))
+    )(*(pltpu.with_memory_space_constraint(x, pltpu.HBM) for x in (pairs.T, dosage, phenotype, perms)))
     return pl.pallas_call(
         functools.partial(statistics, half),
         out_shape=jax.ShapeDtypeStruct((1, kinds, PANEL, half), jnp.bfloat16),
-        in_specs=[vmem, vmem],
+        in_specs=[vmem] * 3,
         out_specs=pl.BlockSpec(memory_space=pl.ANY),
         scratch_shapes=[
             pltpu.VMEM((kinds, PANEL, half), jnp.bfloat16),
-            pltpu.SemaphoreType.DMA((kinds,)),
+            pltpu.SemaphoreType.DMA((kinds * CHUNKS,)),
         ],
         compiler_params=pltpu.CompilerParams(vmem_limit_bytes=min(work_bytes, 60 << 20)),
         name="statistics",
-    )(perms, received)
+    )(*received)
 
 
 def solution(mesh):

time: 11.9 us -> 11.7 us (0.983)
  Pallas kernels: 11.7 us -> 11.5 us
    pallas_call x1, Pallas kernels: 10.1 us -> 9.98 us  [on_device(): pl.pallas_call(functools.partial(exchange, n, samp), out_shape=[jax.Shape...]
where the time goes in v5:
time: 11.7 us; the launch traced here: 11.5 us
  Pallas kernels  11.5 us (98%)
    pallas_call x1, Pallas kernels, on_device(): pl.pallas_call(functools.partial(exchange, n, samp), out_shape=[jax.Shape...  9.98 us
    pallas_call x1, Pallas kernels, on_device(): pl.pallas_call(functools.partial(statistics, half), out_shape=jax.ShapeDt...  1.52 us

profile of v5, /device:TPU:0, one launch (start us, length us, event | category | flops | bytes accessed | tf_op | source)
XLA Modules:
  0.0 11.5 jit_solution(16631821354259888380)
XLA Ops:
  0.0 10.0 %exchange.1 = (bf16[16,4,768]{2,1,0:T(4,128)(2,1)S(1)}, bf16[16,2,128]{2,1,0:T(2,128)(2,1)S(1)}, bf16[2,64,128]{2,1,0:T(8,128)(2,1)S(1)}) custom-call(s32[2,8]{1,0:T(2,128)} %bitcast.1, bf16[4,4096]{1,0:T(4,128)(2,1)} %dosage_hbm.1, bf16[2,4]{1,0:T(2,128)(2,1)} %pheno_hbm.1, s32[2,64]{1,0:T(2,128)} %perms_hbm.1), custom_call_target="tpu_custom_call" | custom-call | tf_op jit(solution)/shard_map/exchange/pallas_call | solution.py:224
  10.0 1.5 %statistics.1 = bf16[1,4,512,256]{3,2,1,0:T(8,128)(2,1)} custom-call(bf16[16,4,768]{2,1,0:T(4,128)(2,1)S(1)} %get-tuple-element.8.recv_ref, bf16[16,2,128]{2,1,0:T(2,128)(2,1)S(1)} %get-tuple-element.9.y_ref, bf16[2,64,128]{2,1,0:T(8,128)(2,1)S(1)} %get-tuple-element.10.hot_ref), custom_call_target="tpu_custom_call" | custom-call | tf_op jit(solution)/shard_map/statistics/pallas_call | solution.py:251

commit v6 on v5

--- a/solution.py
+++ b/solution.py
@@ -24,7 +24,7 @@
 
 def exchange(
     n, samp, pairs_hbm, dosage_hbm, pheno_hbm, perms_hbm, out_ref, y_ref, hot_ref,
-    pairs_ref, perms_ref, dosage_ref, pheno_ref, send_buf, own_y, in_sems, send_sem, recv_sem, y_send, y_recv,
+    pairs_ref, perms_ref, dosage_ref, pheno_ref, send_buf, own_y, in_sems, send_sem, recv_sem, y_send, y_recv, far_sems,
 ):
     half = PANEL // samp
     me = lax.axis_index("pair") * samp + lax.axis_index("samp")
@@ -97,23 +97,40 @@
             send_buf[b * samp + c, :, :PANEL] = geno_a
             send_buf[b * samp + c, :, PANEL : PANEL + half] = geno_b[:, c * half : (c + 1) * half]
 
-    def send(b, c):
+    far = far_sems.shape[0]
+    cells = pl.ds(PANEL, half)
+
+    def reach(b, c, src, dst, sems):
         pltpu.make_async_remote_copy(
-            src_ref=send_buf.at[b * samp + c],
-            dst_ref=out_ref.at[me],
-            send_sem=send_sem,
-            recv_sem=recv_sem,
+            src_ref=src,
+            dst_ref=dst,
+            send_sem=sems[0],
+            recv_sem=sems[1],
             device_id={"pair": b, "samp": c},
             device_id_type=pl.DeviceIdType.MESH,
         ).start()
-        pltpu.make_async_remote_copy(
-            src_ref=own_y,
-            dst_ref=y_ref.at[me],
-            send_sem=y_send,
-            recv_sem=y_recv,
-            device_id={"pair": b, "samp": c},
-            device_id_type=pl.DeviceIdType.MESH,
-        ).start()
+
+    def send(b, c, sem=None):
+        reach(b, c, send_buf.at[b * samp + c], out_ref.at[me], (send_sem, recv_sem if sem is None else sem))
+        reach(b, c, own_y, y_ref.at[me], (y_send, y_recv))
+
+    def send_far(i, b):
+        send(b, samp_me, far_sems.at[i])
+        for c in range(1, samp):
+            other = lax.rem(samp_me + c, samp)
+            slab = send_buf.at[b * samp + other]
+            reach(b, other, slab.at[:, cells], out_ref.at[me, :, cells], (send_sem, recv_sem))
+            reach(b, other, own_y, y_ref.at[me], (y_send, y_recv))
+
+    def pass_on(i, carry):
+        back = i + 1 if pair_n & (pair_n - 1) else pair_n - 1 - i
+        source = partner(pair_me, back, pair_n) * samp + samp_me
+        slab = out_ref.at[source]
+        pltpu.make_async_copy(slab, slab, far_sems.at[i]).wait()
+        row = out_ref.at[source, :, pl.ds(0, PANEL)]
+        for c in range(1, samp):
+            reach(pair_me, lax.rem(samp_me + c, samp), row, row, (send_sem, recv_sem))
+        return carry
 
     fill(0)
     pl.semaphore_wait(barrier, n - 1)
@@ -125,11 +142,17 @@
             send(b, c)
         return carry
 
+    def far_step(i, carry):
+        fill(i + 1)
+        send_far(i, partner(pair_me, pair_n - 1 - i, pair_n))
+        return carry
+
     if small:
         for i in range(pair_n - 1):
-            step(i, 0)
+            (far_step if i < far else step)(i, 0)
     else:
-        lax.fori_loop(0, pair_n - 1, step, 0)
+        lax.fori_loop(0, far, far_step, 0)
+        lax.fori_loop(far, pair_n - 1, step, 0)
     for c in range(1, samp):
         send(pair_me, lax.rem(samp_me + c, samp))
     pltpu.make_async_copy(send_buf.at[me], out_ref.at[me], recv_sem).start()
@@ -142,7 +165,9 @@
         order = jnp.concatenate([order, order], axis=1)
         hot_ref[r] = jnp.where(sample == order, 1.0, 0.0).astype(jnp.bfloat16)
 
-    pltpu.make_async_copy(out_ref, out_ref, recv_sem).wait()
+    lax.fori_loop(0, far, pass_on, 0)
+    landed = out_ref.at[pl.ds(0, n - far)]
+    pltpu.make_async_copy(landed, landed, recv_sem).wait()
     pltpu.make_async_copy(y_ref, y_ref, y_recv).wait()
     for buf, sem in ((send_buf, send_sem), (y_ref, y_send)):
         rest = buf.at[pl.ds(0, n - 1)]
@@ -242,6 +267,7 @@
             pltpu.SemaphoreType.DMA,
             pltpu.SemaphoreType.DMA,
             pltpu.SemaphoreType.DMA,
+            pltpu.SemaphoreType.DMA((max(1, n // samp // 4),)),
         ],
         compiler_params=pltpu.CompilerParams(
             collective_id=0, has_side_effects=True, vmem_limit_bytes=min(kept_bytes, 60 << 20)

time: 11.7 us -> 11.3 us (0.966)
  Pallas kernels: 11.5 us -> 11.2 us
    pallas_call x1, Pallas kernels: 9.98 us -> 9.65 us  [on_device(): pl.pallas_call(functools.partial(exchange, n, samp), out_shape=[jax.Shape...]
where the time goes in v6:
time: 11.3 us; the launch traced here: 11.2 us
  Pallas kernels  11.2 us (99%)
    pallas_call x1, Pallas kernels, on_device(): pl.pallas_call(functools.partial(exchange, n, samp), out_shape=[jax.Shape...  9.65 us
    pallas_call x1, Pallas kernels, on_device(): pl.pallas_call(functools.partial(statistics, half), out_shape=jax.ShapeDt...  1.51 us

profile of v6, /device:TPU:0, one launch (start us, length us, event | category | flops | bytes accessed | tf_op | source)
XLA Modules:
  0.0 11.2 jit_solution(11734121936229760730)
XLA Ops:
  0.0 9.7 %exchange.1 = (bf16[16,4,768]{2,1,0:T(4,128)(2,1)S(1)}, bf16[16,2,128]{2,1,0:T(2,128)(2,1)S(1)}, bf16[2,64,128]{2,1,0:T(8,128)(2,1)S(1)}) custom-call(s32[2,8]{1,0:T(2,128)} %bitcast.1, bf16[4,4096]{1,0:T(4,128)(2,1)} %dosage_hbm.1, bf16[2,4]{1,0:T(2,128)(2,1)} %pheno_hbm.1, s32[2,64]{1,0:T(2,128)} %perms_hbm.1), custom_call_target="tpu_custom_call" | custom-call | tf_op jit(solution)/shard_map/exchange/pallas_call | solution.py:249
  9.7 1.5 %statistics.1 = bf16[1,4,512,256]{3,2,1,0:T(8,128)(2,1)} custom-call(bf16[16,4,768]{2,1,0:T(4,128)(2,1)S(1)} %get-tuple-element.8.recv_ref, bf16[16,2,128]{2,1,0:T(2,128)(2,1)S(1)} %get-tuple-element.9.y_ref, bf16[2,64,128]{2,1,0:T(8,128)(2,1)S(1)} %get-tuple-element.10.hot_ref), custom_call_target="tpu_custom_call" | custom-call | tf_op jit(solution)/shard_map/statistics/pallas_call | solution.py:277

commit v7 on v6

--- a/solution.py
+++ b/solution.py
@@ -116,6 +116,8 @@
 
     def send_far(i, b):
         send(b, samp_me, far_sems.at[i])
+
+    def send_rest(i, b):
         for c in range(1, samp):
             other = lax.rem(samp_me + c, samp)
             slab = send_buf.at[b * samp + other]
@@ -147,11 +149,20 @@
         send_far(i, partner(pair_me, pair_n - 1 - i, pair_n))
         return carry
 
+    def rest_step(i, carry):
+        send_rest(i, partner(pair_me, pair_n - 1 - i, pair_n))
+        return carry
+
     if small:
-        for i in range(pair_n - 1):
-            (far_step if i < far else step)(i, 0)
+        for i in range(far):
+            far_step(i, 0)
+        for i in range(far):
+            rest_step(i, 0)
+        for i in range(far, pair_n - 1):
+            step(i, 0)
     else:
         lax.fori_loop(0, far, far_step, 0)
+        lax.fori_loop(0, far, rest_step, 0)
         lax.fori_loop(far, pair_n - 1, step, 0)
     for c in range(1, samp):
         send(pair_me, lax.rem(samp_me + c, samp))

time: 11.3 us -> 11.3 us (level)
  no operation moved by 1% of the time
where the time goes in v7:
time: 11.3 us; the launch traced here: 11.2 us
  Pallas kernels  11.2 us (99%)
    pallas_call x1, Pallas kernels, on_device(): pl.pallas_call(functools.partial(exchange, n, samp), out_shape=[jax.Shape...  9.65 us
    pallas_call x1, Pallas kernels, on_device(): pl.pallas_call(functools.partial(statistics, half), out_shape=jax.ShapeDt...  1.51 us

profile of v7, /device:TPU:0, one launch (start us, length us, event | category | flops | bytes accessed | tf_op | source)
XLA Modules:
  0.0 11.2 jit_solution(1404369893062987834)
XLA Ops:
  0.0 9.7 %exchange.1 = (bf16[16,4,768]{2,1,0:T(4,128)(2,1)S(1)}, bf16[16,2,128]{2,1,0:T(2,128)(2,1)S(1)}, bf16[2,64,128]{2,1,0:T(8,128)(2,1)S(1)}) custom-call(s32[2,8]{1,0:T(2,128)} %bitcast.1, bf16[4,4096]{1,0:T(4,128)(2,1)} %dosage_hbm.1, bf16[2,4]{1,0:T(2,128)(2,1)} %pheno_hbm.1, s32[2,64]{1,0:T(2,128)} %perms_hbm.1), custom_call_target="tpu_custom_call" | custom-call | tf_op jit(solution)/shard_map/exchange/pallas_call | solution.py:260
  9.7 1.5 %statistics.1 = bf16[1,4,512,256]{3,2,1,0:T(8,128)(2,1)} custom-call(bf16[16,4,768]{2,1,0:T(4,128)(2,1)S(1)} %get-tuple-element.8.recv_ref, bf16[16,2,128]{2,1,0:T(2,128)(2,1)S(1)} %get-tuple-element.9.y_ref, bf16[2,64,128]{2,1,0:T(8,128)(2,1)S(1)} %get-tuple-element.10.hot_ref), custom_call_target="tpu_custom_call" | custom-call | tf_op jit(solution)/shard_map/statistics/pallas_call | solution.py:288
